TPU v7x, 32 devices: a whole 2x2x4 slice. The times are simulated.
32 devices in a mesh: dp: 16 (over z, x, core), tp: 2 (over y).
Axes of the slice: x: 2, y: 2, z: 4, core: 2. Of those that a mesh axis runs over, the one named last changes fastest.
Arguments:
- inputs: bfloat16 [32768, 640], P('dp'), may hold values from -6 to 6
- out_grad: bfloat16 [32768, 640], P('dp'), may hold values from -6 to 6
- segment_ids: int32 [32, 1024], P('dp'), may hold values from 0 to 5, never falling along the last dimension, each value on 1 to 400 neighbouring positions
- attn_weights: float32 [4, 640, 640], P(None, 'dp', 'tp'), may hold values from -6 to 6
- ffn_weights: float32 [2, 640, 2560], P(None, 'dp', 'tp'), may hold values from -4 to 4
- head_bias: float32 [3, 640], P(None, 'tp'), may hold values from -1 to 1
- hidden_bias: float32 [2560], P('tp'), may hold values from -1 to 1
- norm_vectors: float32 [6, 640], replicated, may hold values from -1 to 2
- attn_first: float32 [4, 640, 640], P(None, 'dp', 'tp')
- ffn_first: float32 [2, 640, 2560], P(None, 'dp', 'tp')
- head_first: float32 [3, 640], P(None, 'tp')
- hidden_first: float32 [2560], P('tp')
- vector_first: float32 [6, 640], replicated
- attn_second: float32 [4, 640, 640], P(None, 'dp', 'tp')
- ffn_second: float32 [2, 640, 2560], P(None, 'dp', 'tp')
- head_second: float32 [3, 640], P(None, 'tp')
- hidden_second: float32 [2560], P('tp')
- vector_second: float32 [6, 640], replicated
Outputs:
- layer_output: bfloat16 [32768, 640], P('dp')
- input_grad: bfloat16 [32768, 640], P('dp')
- new_attn_weights: float32 [4, 640, 640], P(None, 'dp', 'tp')
- new_ffn_weights: float32 [2, 640, 2560], P(None, 'dp', 'tp')
- new_head_bias: float32 [3, 640], P(None, 'tp')
- new_hidden_bias: float32 [2560], P('tp')
- new_norm_vectors: float32 [6, 640], replicated
- attn_first_new: float32 [4, 640, 640], P(None, 'dp', 'tp')
- ffn_first_new: float32 [2, 640, 2560], P(None, 'dp', 'tp')
- head_first_new: float32 [3, 640], P(None, 'tp')
- hidden_first_new: float32 [2560], P('tp')
- vector_first_new: float32 [6, 640], replicated
- attn_second_new: float32 [3, 640, 640], P(None, 'dp', 'tp')
- out_second_new: float32 [640, 640], P('dp', 'tp')
- ffn_second_new: float32 [2, 640, 2560], P(None, 'dp', 'tp')
- head_second_new: float32 [3, 640], P(None, 'tp')
- hidden_second_new: float32 [2560], P('tp')
- vector_second_new: float32 [4, 640], replicated
- norm_second_new: float32 [2, 640], replicated
- trust_norms: float32 [2, 16], replicated
Inputs may be any that keep to these rules, and one draw needn't show every extreme that they name: `segment_ids`: within each row of 1024 slots the ids never fall; each of the 6 ids forms one run of 1 to 400 slots, and one run has exactly 400 slots.
All inputs are finite; a program needn't handle non-finite values.
Results may differ from a plain program's by a relative error of at most 0.019.
Values may be sent and summed in bfloat16 or wider, within the bound.
No kernel may reach another device: no remote copies, remote signals or barrier semaphores. Data moves between devices by JAX's collectives and lax.ppermute only.
A program may use at most 192 MiB of HBM per device.

v0:
```python
from functools import partial
import jax
import jax.numpy as jnp
from jax import lax
from jax.sharding import PartitionSpec as P

HD = 32
STEP = 10
EPS_NORM = 1e-05
EPS_ADAM = 1e-06
BETA_ONE = 0.9
BETA_TWO = 0.999
DECAY = 0.01
RATE = 0.5
MASKED = -1e30


def layer_norm(values, scale_gain, offset):
    average = jnp.mean(values, axis=-1, keepdims=True)
    centered = values - average
    variance = jnp.mean(centered * centered, axis=-1, keepdims=True)
    return centered * lax.rsqrt(variance + EPS_NORM) * scale_gain + offset


def rope_tables(segments):
    slots_index = jnp.arange(segments.shape[0], dtype=jnp.int32)
    before = jnp.sum((segments[None, :] < segments[:, None]).astype(jnp.int32), axis=1)
    position = (slots_index - before).astype(jnp.float32)
    frequency = 10000.0 ** (-jnp.arange(0, HD, 2).astype(jnp.float32) / HD)
    angles = position[:, None] * frequency[None, :]
    angles = jnp.concatenate([angles, angles], axis=-1)
    return (jnp.cos(angles), jnp.sin(angles))


def rotate(values, cosine_table, sine_table):
    middle = values.shape[-1] // 2
    turned = jnp.concatenate([-values[..., middle:], values[..., :middle]], axis=-1)
    return values * cosine_table + turned * sine_table


def block_scores(queries, keys_row, same_protein):
    scores = jnp.einsum(
        "qhd,khd->hqk", queries, keys_row, preferred_element_type=jnp.float32
    ) * HD ** (-0.5)
    return jnp.where(same_protein[None], scores, MASKED)


def attend_block(queries, keys_row, values_row, same_protein):
    scores = block_scores(queries, keys_row, same_protein)
    highest = jnp.max(scores, axis=-1, keepdims=True)
    weights_exp = jnp.exp(scores - highest)
    row_total = jnp.sum(weights_exp, axis=-1, keepdims=True)
    attention = (weights_exp / row_total).astype(jnp.bfloat16)
    heads_out = jnp.einsum(
        "hqk,khd->qhd", attention, values_row, preferred_element_type=jnp.float32
    )
    return (heads_out, (highest + jnp.log(row_total))[..., 0])


def attend_block_back(queries, keys_row, values_row, same_protein, log_total, grad_heads):
    scores = block_scores(queries, keys_row, same_protein)
    attention = jnp.exp(scores - log_total[..., None])
    grad_values = jnp.einsum(
        "hqk,qhd->khd",
        attention.astype(jnp.bfloat16),
        grad_heads,
        preferred_element_type=jnp.float32,
    )
    grad_attention = jnp.einsum(
        "qhd,khd->hqk", grad_heads, values_row, preferred_element_type=jnp.float32
    )
    center = jnp.sum(attention * grad_attention, axis=-1, keepdims=True)
    grad_scores = (attention * (grad_attention - center)).astype(jnp.bfloat16)
    grad_queries = jnp.einsum(
        "hqk,khd->qhd", grad_scores, keys_row, preferred_element_type=jnp.float32
    ) * HD ** (-0.5)
    grad_keys = jnp.einsum(
        "hqk,qhd->khd", grad_scores, queries, preferred_element_type=jnp.float32
    ) * HD ** (-0.5)
    return (grad_queries, grad_keys, grad_values)


def attend_row(queries, keys_row, values_row, segments, block_rows):
    blocks = segments.shape[0] // block_rows
    query_blocks = queries.reshape((blocks, block_rows) + queries.shape[1:])
    segment_blocks = segments.reshape(blocks, block_rows)

    def one_block(packed):
        same_protein = packed[1][:, None] == segments[None, :]
        return attend_block(packed[0], keys_row, values_row, same_protein)

    heads_out, log_total = lax.map(one_block, (query_blocks, segment_blocks))
    return (heads_out.reshape(queries.shape), log_total)


def attend_row_back(queries, keys_row, values_row, segments, log_total, grad_heads, block_rows):
    blocks = segments.shape[0] // block_rows
    query_blocks = queries.reshape((blocks, block_rows) + queries.shape[1:])
    grad_blocks = grad_heads.reshape((blocks, block_rows) + grad_heads.shape[1:])
    segment_blocks = segments.reshape(blocks, block_rows)

    def one_block(totals, packed):
        same_protein = packed[1][:, None] == segments[None, :]
        grad_queries, grad_keys, grad_values = attend_block_back(
            packed[0], keys_row, values_row, same_protein, packed[2], packed[3]
        )
        return ((totals[0] + grad_keys, totals[1] + grad_values), grad_queries)

    zeros_rows = jnp.zeros(keys_row.shape, jnp.float32)
    sums_kv, grad_queries = lax.scan(
        one_block, (zeros_rows, zeros_rows), (query_blocks, segment_blocks, log_total, grad_blocks)
    )
    return (grad_queries.reshape(queries.shape), sums_kv[0], sums_kv[1])


def lamb_moments(weight, gradient, moment_one, moment_two):
    first_new = BETA_ONE * moment_one + (1.0 - BETA_ONE) * gradient
    second_new = BETA_TWO * moment_two + (1.0 - BETA_TWO) * gradient * gradient
    corrected = first_new / (1.0 - BETA_ONE**STEP)
    variance = second_new / (1.0 - BETA_TWO**STEP)
    update = corrected / (jnp.sqrt(variance) + EPS_ADAM) + DECAY * weight
    return (first_new, second_new, update)


def sum_squares(array):
    return jnp.sum(array * array, axis=tuple(range(1, array.ndim)))


def on_device(
    inputs,
    out_grad,
    segment_ids,
    attn_weights,
    ffn_weights,
    head_bias,
    hidden_bias,
    norm_vectors,
    attn_first,
    ffn_first,
    head_first,
    hidden_first,
    vector_first,
    attn_second,
    ffn_second,
    head_second,
    hidden_second,
    vector_second,
):
    data_count = lax.axis_size("dp")
    tensor_count = lax.axis_size("tp")
    row_count, slot_count = segment_ids.shape
    token_count = row_count * slot_count
    head_width = attn_weights.shape[2]
    local_heads = head_width // HD
    block_rows = min(512, slot_count)
    shard_rows = attn_weights.shape[1]
    masters = [attn_weights, ffn_weights, head_bias, hidden_bias.reshape(1, -1), norm_vectors]
    replicas = [1.0, 1.0, 1.0 / data_count, 1.0 / data_count, 1.0 / (data_count * tensor_count)]
    weight_terms = jnp.concatenate(
        [sum_squares(masters[member]) * replicas[member] for member in range(5)]
    )
    weight_sums = lax.psum(weight_terms, ("dp", "tp"))
    gathered_attn, gathered_ffn = (
        lax.all_gather(attn_weights.astype(jnp.bfloat16), "dp", axis=1, tiled=True),
        lax.all_gather(ffn_weights.astype(jnp.bfloat16), "dp", axis=1, tiled=True),
    )
    tables = jax.vmap(rope_tables)(segment_ids)
    cosine_table = tables[0][:, :, None, :]
    sine_table = tables[1][:, :, None, :]
    features = inputs.astype(jnp.float32)
    normed, norm_back = jax.vjp(layer_norm, features, norm_vectors[0], norm_vectors[1])
    normed_low = normed.astype(jnp.bfloat16)
    projected = jnp.einsum(
        "td,cdw->ctw", normed_low, gathered_attn[:3], preferred_element_type=jnp.float32
    )
    projected = projected + head_bias[:, None, :]
    shaped = projected.reshape(3, row_count, slot_count, local_heads, HD)
    turned, rotate_back = jax.vjp(lambda pair: rotate(pair, cosine_table, sine_table), shaped[:2])
    turned_low = turned.astype(jnp.bfloat16)
    values_low = shaped[2].astype(jnp.bfloat16)
    heads_out, log_total = lax.map(
        lambda packed: attend_row(packed[0], packed[1], packed[2], packed[3], block_rows),
        (turned_low[0], turned_low[1], values_low, segment_ids),
    )
    heads_low = heads_out.reshape(token_count, head_width).astype(jnp.bfloat16)
    out_projection = gathered_attn[3]
    attended = lax.psum(
        jnp.einsum(
            "tw,dw->td", heads_low, out_projection, preferred_element_type=jnp.float32
        ).astype(jnp.bfloat16),
        "tp",
    ).astype(jnp.float32)
    residual = features + attended + norm_vectors[2]
    normed_two, norm_two_back = jax.vjp(layer_norm, residual, norm_vectors[3], norm_vectors[4])
    normed_two_low = normed_two.astype(jnp.bfloat16)
    preact = (
        jnp.dot(normed_two_low, gathered_ffn[0], preferred_element_type=jnp.float32) + hidden_bias
    )
    activated, gelu_back = jax.vjp(partial(jax.nn.gelu, approximate=False), preact)
    activated_low = activated.astype(jnp.bfloat16)
    mixed_sum = lax.psum(
        jnp.einsum(
            "tf,df->td", activated_low, gathered_ffn[1], preferred_element_type=jnp.float32
        ).astype(jnp.bfloat16),
        "tp",
    ).astype(jnp.float32)
    layer_output = (residual + mixed_sum + norm_vectors[5]).astype(jnp.bfloat16)
    grad_output = out_grad.astype(jnp.float32)
    grad_down = jnp.einsum("td,tf->df", out_grad, activated_low, preferred_element_type=jnp.float32)
    grad_act = jnp.einsum(
        "td,df->tf", out_grad, gathered_ffn[1], preferred_element_type=jnp.float32
    )
    grad_pre = gelu_back(grad_act)[0].astype(jnp.bfloat16)
    grad_up = jnp.einsum("td,tf->df", normed_two_low, grad_pre, preferred_element_type=jnp.float32)
    grad_hidden_bias = jnp.sum(grad_pre.astype(jnp.float32), axis=0)
    grad_normed_two = lax.psum(
        jnp.einsum(
            "tf,df->td", grad_pre, gathered_ffn[0], preferred_element_type=jnp.float32
        ).astype(jnp.bfloat16),
        "tp",
    ).astype(jnp.float32)
    grad_residual_ln, grad_gain_two, grad_shift_two = norm_two_back(grad_normed_two)
    grad_residual = grad_output + grad_residual_ln
    grad_residual_low = grad_residual.astype(jnp.bfloat16)
    grad_out_projection = jnp.einsum(
        "td,tw->dw", grad_residual_low, heads_low, preferred_element_type=jnp.float32
    )
    grad_heads = jnp.einsum(
        "td,dw->tw", grad_residual_low, out_projection, preferred_element_type=jnp.float32
    )
    grad_heads = grad_heads.astype(jnp.bfloat16).reshape(row_count, slot_count, local_heads, HD)
    grad_turned_q, grad_turned_k, grad_values = lax.map(
        lambda packed: attend_row_back(
            packed[0], packed[1], packed[2], packed[3], packed[4], packed[5], block_rows
        ),
        (turned_low[0], turned_low[1], values_low, segment_ids, log_total, grad_heads),
    )
    grad_shaped_qk = rotate_back(jnp.stack([grad_turned_q, grad_turned_k]))[0]
    grad_projected = jnp.concatenate([grad_shaped_qk, grad_values[None]], axis=0)
    grad_projected = grad_projected.reshape(3, token_count, head_width).astype(jnp.bfloat16)
    grad_head_bias = jnp.sum(grad_projected.astype(jnp.float32), axis=1)
    grad_qkv = jnp.einsum(
        "td,ctw->cdw", normed_low, grad_projected, preferred_element_type=jnp.float32
    )
    grad_normed = lax.psum(
        jnp.einsum(
            "ctw,cdw->td", grad_projected, gathered_attn[:3], preferred_element_type=jnp.float32
        ).astype(jnp.bfloat16),
        "tp",
    ).astype(jnp.float32)
    grad_features_ln, grad_gain, grad_shift = norm_back(grad_normed)
    input_grad = (grad_residual + grad_features_ln).astype(jnp.bfloat16)
    grad_vectors = jnp.stack(
        [
            grad_gain,
            grad_shift,
            jnp.sum(grad_residual, axis=0),
            grad_gain_two,
            grad_shift_two,
            jnp.sum(grad_output, axis=0),
        ]
    )
    grad_attn = jnp.concatenate([grad_qkv, grad_out_projection[None]], axis=0)
    grad_ffn = jnp.stack([grad_up, grad_down])
    full_attn, full_ffn, sum_head, sum_hidden, sum_vectors = lax.psum(
        (grad_attn, grad_ffn, grad_head_bias, grad_hidden_bias, grad_vectors), "dp"
    )
    offset_rows = lax.axis_index("dp") * shard_rows
    own_attn = lax.dynamic_slice_in_dim(full_attn, offset_rows, shard_rows, 1)
    own_ffn = lax.dynamic_slice_in_dim(full_ffn, offset_rows, shard_rows, 1)
    grads_list = [own_attn, own_ffn, sum_head, sum_hidden.reshape(1, -1), sum_vectors]
    firsts = [attn_first, ffn_first, head_first, hidden_first.reshape(1, -1), vector_first]
    seconds = [attn_second, ffn_second, head_second, hidden_second.reshape(1, -1), vector_second]
    results = [
        lamb_moments(masters[member], grads_list[member], firsts[member], seconds[member])
        for member in range(5)
    ]
    update_terms = jnp.concatenate(
        [sum_squares(results[member][2]) * replicas[member] for member in range(5)]
    )
    update_sums = lax.psum(update_terms, ("dp", "tp"))
    weight_norms = jnp.sqrt(weight_sums)
    update_norms = jnp.sqrt(update_sums)
    trust_ratio = weight_norms / update_norms
    counts = [4, 2, 3, 1, 6]
    new_weights = []
    begin_at = 0
    for member in range(5):
        piece_ratio = trust_ratio[begin_at : begin_at + counts[member]]
        shaped_ratio = piece_ratio.reshape((-1,) + (1,) * (masters[member].ndim - 1))
        new_weights.append(masters[member] - RATE * shaped_ratio * results[member][2])
        begin_at += counts[member]
    return (
        layer_output,
        input_grad,
        new_weights[0],
        new_weights[1],
        new_weights[2],
        new_weights[3].reshape(-1),
        new_weights[4],
        results[0][0],
        results[1][0],
        results[2][0],
        results[3][0].reshape(-1),
        results[4][0],
        results[0][1][:3],
        results[0][1][3],
        results[1][1],
        results[2][1],
        results[3][1].reshape(-1),
        results[4][1][2:],
        results[4][1][:2],
        jnp.stack([weight_norms, update_norms]),
    )


def solution(mesh):
    in_specs = (
        P("dp", None),
        P("dp", None),
        P("dp", None),
        P(None, "dp", "tp"),
        P(None, "dp", "tp"),
        P(None, "tp"),
        P("tp"),
        P(),
        P(None, "dp", "tp"),
        P(None, "dp", "tp"),
        P(None, "tp"),
        P("tp"),
        P(),
        P(None, "dp", "tp"),
        P(None, "dp", "tp"),
        P(None, "tp"),
        P("tp"),
        P(),
    )
    out_specs = (
        P("dp", None),
        P("dp", None),
        P(None, "dp", "tp"),
        P(None, "dp", "tp"),
        P(None, "tp"),
        P("tp"),
        P(),
        P(None, "dp", "tp"),
        P(None, "dp", "tp"),
        P(None, "tp"),
        P("tp"),
        P(),
        P(None, "dp", "tp"),
        P("dp", "tp"),
        P(None, "dp", "tp"),
        P(None, "tp"),
        P("tp"),
        P(),
        P(),
        P(),
    )
    return jax.shard_map(
        on_device, mesh=mesh, in_specs=in_specs, out_specs=out_specs, check_vma=False
    )
```

profile of v0, /device:TPU:12, one launch (start us, length us, event | category | flops | bytes accessed | tf_op | source)
XLA Modules:
  0.0 1304.4 jit_solution(11081138493760027001)
XLA Ops:
  17.8 34.1 %all-gather.3.cloned.1.call-done = bf16[4,640,320]{2,0,1:T(4,128)(2,1)} async-done(((bf16[4,40,320]{2,0,1:T(4,128)(2,1)}), bf16[4,640,320]{2,0,1:T(4,128)(2,1)}) %all-gather.3.cloned.1.call-update) | async-done | bytes 1638416 | tf_op jit(solution)/shard_map/all_gather | solution.py:164
  67.5 8.1 slice.89
  88.0 138.8 %while.54 = (s32[]{:T(128)}, bf16[2,1024,10,32]{3,2,1,0:T(8,128)(2,1)}, f32[2,2,10,512]{3,2,1,0:T(8,128)}, bf16[2,1024,10,32]{1,3,2,0:T(8,128)(2,1)S(1)}, s32[2,...) while((s32[]{:T(128)}, ...), condition=%wide.region_8.0_spmd, body=%wide.region_3.8_spmd.sunk | while | flops 734522368 | bytes 181594624 | solution.py:181
  92.8 54.8 %while.57 = (s32[]{:T(128)}, bf16[2,512,10,32]{1,3,2,0:T(8,128)(2,1)S(1)}, f32[2,10,512]{2,1,0:T(8,128)S(1)}, s32[2,512]{1,0:T(2,128)S(1)}, s32[1024]{0:T(1024)S...) while((s32[]{:T(128)}, ...), condition=%wide.region_7.7_spmd, body=%wide.region_4.6_spmd.sunk | while | flops 734522368 | bytes 154048688 | solution.py:92
  97.3 7.0 copy-done.1
  104.2 6.2 fusion.156
  110.5 9.7 fusion.157
  124.7 7.0 copy-done.1
  131.6 6.2 fusion.156
  137.9 9.7 fusion.157
  162.2 54.8 %while.57 = (s32[]{:T(128)}, bf16[2,512,10,32]{1,3,2,0:T(8,128)(2,1)S(1)}, f32[2,10,512]{2,1,0:T(8,128)S(1)}, s32[2,512]{1,0:T(2,128)S(1)}, s32[1024]{0:T(1024)S...) while((s32[]{:T(128)}, ...), condition=%wide.region_7.7_spmd, body=%wide.region_4.6_spmd.sunk | while | flops 734522368 | bytes 154048688 | solution.py:92
  166.6 7.0 copy-done.1
  173.6 6.2 fusion.156
  179.8 9.7 fusion.157
  194.0 7.0 copy-done.1
  207.2 9.7 fusion.157
  227.8 10.1 reshape.337
  243.5 72.7 %all-reduce.11.cloned.1.call-done = bf16[2048,640]{1,0:T(8,128)(2,1)} async-done(((bf16[2048,640]{1,0:T(8,128)(2,1)}), bf16[2048,640]{1,0:T(8,128)(2,1)}) %all-reduce.11.cloned.1.call-update) | async-done | bytes 2621456 | tf_op jit(solution)/shard_map/psum | solution.py:187
  320.5 46.1 %all-gather.5.cloned.1.call-done = bf16[2,640,1280]{2,1,0:T(8,128)(2,1)} async-done(((bf16[2,40,1280]{2,1,0:T(8,128)(2,1)}), bf16[2,640,1280]{2,1,0:T(8,128)(2,1)}) %all-gather.5.cloned.1.call-update) | async-done | bytes 3276816 | tf_op jit(solution)/shard_map/all_gather | solution.py:165
  366.6 31.1 %multiply_convert_fusion.1 = (bf16[2048,1280]{1,0:T(8,128)(2,1)}, f32[2048,1280]{1,0:T(8,128)}, f32[2048,1280]{1,0:T(8,128)}) fusion(f32[1280]{0:T(1024)S(1)} %copy-done.50, bf16[2,640,1280]{2,1,0:T(8,128)(2,1)} %all-gather.5.cloned.1.call-done, f32[640]{0:T(1024)S(1)} %copy-done.58, f32[640]{0:T(1024)S(1)} %copy-done.47, f32[2048]{0:T(1024)S(1)} %fusion.84, ...), kind=kOutput, calls=%fused_computation.69 | convolution fusion | flops 3540254720 | bytes 33124864 | tf_op jit(solution)/shard_map/dot_general | solution.py:197
  397.8 12.4 convert_reduce_fusion
  418.6 7.3 convolution_bitcast_fusion
  433.5 56.9 %all-reduce.13.cloned.1.call-done = bf16[2048,640]{1,0:T(8,128)(2,1)} async-done(((bf16[2048,640]{1,0:T(8,128)(2,1)}), bf16[2048,640]{1,0:T(8,128)(2,1)}) %all-reduce.13.cloned.1.call-update) | async-done | bytes 2621456 | tf_op jit(solution)/shard_map/psum | solution.py:216
  510.4 277.2 %while.56 = (s32[]{:T(128)}, f32[2,1024,10,32]{1,3,2,0:T(8,128)}, f32[2,1024,10,32]{1,3,2,0:T(8,128)}, bf16[2,1024,10,32]{1,3,2,0:T(8,128)(2,1)}, bf16[2,1024,10...) while((s32[]{:T(128)}, f32[2,1024,10,32]{1,3,2,0:T(8,128)}, ...), condition=%wide.region_20.21_spmd, body=%wide.region_16.20_spmd.sunk | while | flops 1758686208 | bytes 284158464 | solution.py:232
  522.2 111.2 %while.58 = (s32[]{:T(128)}, f32[1024,10,32]{0,2,1:T(8,128)S(1)}, f32[1024,10,32]{0,2,1:T(8,128)}, f32[2,512,10,32]{1,3,2,0:T(8,128)}, bf16[2,512,10,32]{1,3,2,0...) while((s32[]{:T(128)}, f32[1024,10,32]{0,2,1:T(8,128)S(1)}, ...), condition=%wide.region_19.19_spmd.clone, body=%wide.region_17.18_spmd.clone.sunk | while | flops 1758686208 | bytes 255219920 | solution.py:110
  527.2 7.0 copy-done
  534.2 7.7 fusion.151
  541.9 15.2 %multiply_reduce_fusion.13 = (f32[10,512]{1,0:T(8,128)S(1)}, f32[10,512,1024]{2,1,0:T(8,128)}) fusion(f32[10,512,1024]{2,1,0:T(8,128)} %copy-done, f32[10,512]{1,0:T(8,128)S(1)} %dynamic-slice_bitcast_fusion.15, pred[512,1024]{1,0:T(8,128)(4,1)S(1)} %broadcast_compare_fusion.4, bf16[1024,10,32]{0,2,1:T(8,128)(2,1)} %get-tuple-element.1035, ...), kind=kOutput, calls=%fused_computation.18.clone.1 | convolution fusion | flops 361753600 | bytes 43491332 | tf_op jit(solution)/shard_map/while/body/eval_jaxpr/while/body/eval_jaxpr/qhd,khd->hqk/dot_general | solution.py:69
  557.0 14.6 %multiply_convert_fusion.3 = bf16[10,512,1024]{2,1,0:T(8,128)(2,1)S(1)} fusion(f32[10,512,1024]{2,1,0:T(8,128)} %get-tuple-element.987, f32[10,512,1024]{2,1,0:T(8,128)} %copy-done, f32[10,512]{1,0:T(8,128)S(1)} %get-tuple-element.988, f32[10,512]{1,0:T(8,128)S(1)} %dynamic-slice_bitcast_fusion.15, pred[512,1024]{1,0:T(8,128)(4,1)S(1)} %broadcast_compare_fusion.4), kind=kLoop, calls=%fused_computation.17.clone.1 | loop fusion | flops 31457280 | bytes 52994048 | tf_op jit(solution)/shard_map/while/body/eval_jaxpr/while/body/eval_jaxpr/convert_element_type | solution.py:73
  582.7 7.0 copy-done
  589.7 7.9 fusion.151
  597.6 15.2 %multiply_reduce_fusion.13 = (f32[10,512]{1,0:T(8,128)S(1)}, f32[10,512,1024]{2,1,0:T(8,128)}) fusion(f32[10,512,1024]{2,1,0:T(8,128)} %copy-done, f32[10,512]{1,0:T(8,128)S(1)} %dynamic-slice_bitcast_fusion.15, pred[512,1024]{1,0:T(8,128)(4,1)S(1)} %broadcast_compare_fusion.4, bf16[1024,10,32]{0,2,1:T(8,128)(2,1)} %get-tuple-element.1035, ...), kind=kOutput, calls=%fused_computation.18.clone.1 | convolution fusion | flops 361753600 | bytes 43491332 | tf_op jit(solution)/shard_map/while/body/eval_jaxpr/while/body/eval_jaxpr/qhd,khd->hqk/dot_general | solution.py:69
  612.8 14.6 %multiply_convert_fusion.3 = bf16[10,512,1024]{2,1,0:T(8,128)(2,1)S(1)} fusion(f32[10,512,1024]{2,1,0:T(8,128)} %get-tuple-element.987, f32[10,512,1024]{2,1,0:T(8,128)} %copy-done, f32[10,512]{1,0:T(8,128)S(1)} %get-tuple-element.988, f32[10,512]{1,0:T(8,128)S(1)} %dynamic-slice_bitcast_fusion.15, pred[512,1024]{1,0:T(8,128)(4,1)S(1)} %broadcast_compare_fusion.4), kind=kLoop, calls=%fused_computation.17.clone.1 | loop fusion | flops 31457280 | bytes 52994048 | tf_op jit(solution)/shard_map/while/body/eval_jaxpr/while/body/eval_jaxpr/convert_element_type | solution.py:73
  660.5 111.2 %while.58 = (s32[]{:T(128)}, f32[1024,10,32]{0,2,1:T(8,128)S(1)}, f32[1024,10,32]{0,2,1:T(8,128)}, f32[2,512,10,32]{1,3,2,0:T(8,128)}, bf16[2,512,10,32]{1,3,2,0...) while((s32[]{:T(128)}, f32[1024,10,32]{0,2,1:T(8,128)S(1)}, ...), condition=%wide.region_19.19_spmd.clone, body=%wide.region_17.18_spmd.clone.sunk | while | flops 1758686208 | bytes 255219920 | solution.py:110
  665.5 7.0 copy-done
  672.5 7.7 fusion.151
  680.2 15.2 %multiply_reduce_fusion.13 = (f32[10,512]{1,0:T(8,128)S(1)}, f32[10,512,1024]{2,1,0:T(8,128)}) fusion(f32[10,512,1024]{2,1,0:T(8,128)} %copy-done, f32[10,512]{1,0:T(8,128)S(1)} %dynamic-slice_bitcast_fusion.15, pred[512,1024]{1,0:T(8,128)(4,1)S(1)} %broadcast_compare_fusion.4, bf16[1024,10,32]{0,2,1:T(8,128)(2,1)} %get-tuple-element.1035, ...), kind=kOutput, calls=%fused_computation.18.clone.1 | convolution fusion | flops 361753600 | bytes 43491332 | tf_op jit(solution)/shard_map/while/body/eval_jaxpr/while/body/eval_jaxpr/qhd,khd->hqk/dot_general | solution.py:69
  695.3 14.6 %multiply_convert_fusion.3 = bf16[10,512,1024]{2,1,0:T(8,128)(2,1)S(1)} fusion(f32[10,512,1024]{2,1,0:T(8,128)} %get-tuple-element.987, f32[10,512,1024]{2,1,0:T(8,128)} %copy-done, f32[10,512]{1,0:T(8,128)S(1)} %get-tuple-element.988, f32[10,512]{1,0:T(8,128)S(1)} %dynamic-slice_bitcast_fusion.15, pred[512,1024]{1,0:T(8,128)(4,1)S(1)} %broadcast_compare_fusion.4), kind=kLoop, calls=%fused_computation.17.clone.1 | loop fusion | flops 31457280 | bytes 52994048 | tf_op jit(solution)/shard_map/while/body/eval_jaxpr/while/body/eval_jaxpr/convert_element_type | solution.py:73
  721.0 7.0 copy-done
  728.0 7.9 fusion.151
  735.9 15.2 %multiply_reduce_fusion.13 = (f32[10,512]{1,0:T(8,128)S(1)}, f32[10,512,1024]{2,1,0:T(8,128)}) fusion(f32[10,512,1024]{2,1,0:T(8,128)} %copy-done, f32[10,512]{1,0:T(8,128)S(1)} %dynamic-slice_bitcast_fusion.15, pred[512,1024]{1,0:T(8,128)(4,1)S(1)} %broadcast_compare_fusion.4, bf16[1024,10,32]{0,2,1:T(8,128)(2,1)} %get-tuple-element.1035, ...), kind=kOutput, calls=%fused_computation.18.clone.1 | convolution fusion | flops 361753600 | bytes 43491332 | tf_op jit(solution)/shard_map/while/body/eval_jaxpr/while/body/eval_jaxpr/qhd,khd->hqk/dot_general | solution.py:69
  751.1 14.6 %multiply_convert_fusion.3 = bf16[10,512,1024]{2,1,0:T(8,128)(2,1)S(1)} fusion(f32[10,512,1024]{2,1,0:T(8,128)} %get-tuple-element.987, f32[10,512,1024]{2,1,0:T(8,128)} %copy-done, f32[10,512]{1,0:T(8,128)S(1)} %get-tuple-element.988, f32[10,512]{1,0:T(8,128)S(1)} %dynamic-slice_bitcast_fusion.15, pred[512,1024]{1,0:T(8,128)(4,1)S(1)} %broadcast_compare_fusion.4), kind=kLoop, calls=%fused_computation.17.clone.1 | loop fusion | flops 31457280 | bytes 52994048 | tf_op jit(solution)/shard_map/while/body/eval_jaxpr/while/body/eval_jaxpr/convert_element_type | solution.py:73
  817.2 8.9 convolution_convert_fusion.1
  837.5 182.1 %all-reduce.15.cloned.1.call-done = (f32[4,640,320]{2,1,0:T(8,128)}, f32[2,640,1280]{2,1,0:T(8,128)}) async-done(((f32[4,640,320]{2,1,0:T(8,128)}, f32[2,640,1280]{2,1,0:T(8,128)}), (f32[4,640,320]{2,1,0:T(8,128)}, f32[2,640,1280]{2,1,0:T(8,128)})) %all-reduce.15.cloned.1.call-update) | async-done | bytes 9830416 | tf_op jit(solution)/shard_map/psum | solution.py:265
  1025.9 126.9 %all-reduce.17.cloned.1.call-done = (bf16[2048,640]{1,0:T(8,128)(2,1)}, bf16[2048,640]{1,0:T(8,128)(2,1)}) async-done(((bf16[2048,640]{1,0:T(8,128)(2,1)}, bf16[2048,640]{1,0:T(8,128)(2,1)}), (bf16[2048,640]{1,0:T(8,128)(2,1)}, bf16[2048,640]{1,0:T(8,128)(2,1)})) %all-reduce.17.cloned.1.call-update) | async-done | bytes 5242896 | tf_op jit(solution)/shard_map/psum | solution.py:201
  1161.9 54.0 %all-reduce.3 = (f32[3,320]{1,0:T(4,128)}, f32[1280]{0:T(1024)}, f32[6,640]{1,0:T(8,128)}) all-reduce(f32[3,320]{1,0:T(4,128)} %convert_reduce_fusion.2, f32[1280]{0:T(1024)} %get-tuple-element.699, f32[6,640]{1,0:T(8,128)S(1)} %stack.48), channel_id=1, replica_groups=mesh['dp'=16,'tp'=2] {'dp'}, use_global_device_ids=true, to_apply=%region_35.36 | all-reduce | flops 6080 | bytes 48640 | tf_op jit(solution)/shard_map/psum | solution.py:265
  1226.4 48.9 %all-reduce.2 = (f32[16]{0:T(128)}, f32[16]{0:T(128)}) all-reduce(f32[16]{0:T(128)} %concatenate.39, f32[16]{0:T(128)} %concatenate.37), channel_id=1, replica_groups=mesh['dp'=16,'tp'=2] {'dp','tp'}, use_global_device_ids=true, to_apply=%region_48.49 | all-reduce | flops 32 | bytes 256 | tf_op jit(solution)/shard_map/psum | solution.py:281
  1288.0 9.4 add_convert_fusion.1
  (365 shorter events, 313.7 us)
Async XLA Ops:
  7.2 9.0 copy-start.3
  7.2 49.2 %copy-start.51 = (f32[3,320]{1,0:T(4,128)S(1)}, f32[3,320]{1,0:T(4,128)}, u32[]{:S(2)}) copy-start(f32[3,320]{1,0:T(4,128)} %param.31) | copy-start | bytes 11524
  7.2 44.7 %all-gather.3.cloned.1.call-start = ((), (), s32[]{:S(2)}) async-start(), calls=%async_computation | async-start | bytes 2088960 | tf_op jit(solution)/shard_map/all_gather | solution.py:164
  9.1 307.1 %all-reduce.11.cloned.1.call-start = ((), (), s32[]{:S(2)}) async-start(), calls=%async_computation.1 | async-start | bytes 5242880 | tf_op jit(solution)/shard_map/psum | solution.py:187
  10.8 50.4 %copy-start.48 = (f32[640]{0:T(1024)}, f32[640]{0:T(1024)S(1)}, u32[]{:S(2)}) copy-start(f32[640]{0:T(1024)S(1)} %get-tuple-element.571) | copy-start | bytes 7684
  10.8 50.4 %copy-start.56 = (f32[640]{0:T(1024)}, f32[640]{0:T(1024)S(1)}, u32[]{:S(2)}) copy-start(f32[640]{0:T(1024)S(1)} %get-tuple-element.570) | copy-start | bytes 7684
  13.8 69.5 %copy-start.29 = (f32[2,1024,32]{1,2,0:T(8,128)}, f32[2,1024,32]{1,2,0:T(8,128)S(1)}, u32[]{:S(2)}) copy-start(f32[2,1024,32]{1,2,0:T(8,128)S(1)} %get-tuple-element.692) | copy-start | bytes 786436
  13.8 69.5 %copy-start.31 = (f32[2,1024,32]{1,2,0:T(8,128)}, f32[2,1024,32]{1,2,0:T(8,128)S(1)}, u32[]{:S(2)}) copy-start(f32[2,1024,32]{1,2,0:T(8,128)S(1)} %get-tuple-element.693) | copy-start | bytes 786436
  16.2 45.1 %copy-start.38 = (f32[2048]{0:T(1024)}, f32[2048]{0:T(1024)S(1)}, u32[]{:S(2)}) copy-start(f32[2048]{0:T(1024)S(1)} %broadcast_multiply_fusion.2) | copy-start | bytes 24580
  17.8 43.4 %copy-start.43 = (f32[2048]{0:T(1024)}, f32[2048]{0:T(1024)S(1)}, u32[]{:S(2)}) copy-start(f32[2048]{0:T(1024)S(1)} %fusion.83) | copy-start | bytes 24580
  92.8 54.8 %copy-start.36 = (f32[2,2,10,512]{3,2,1,0:T(8,128)S(1)}, f32[2,2,10,512]{3,2,1,0:T(8,128)}, u32[]{:S(2)}) copy-start(f32[2,2,10,512]{3,2,1,0:T(8,128)} %get-tuple-element.1077) | copy-start | bytes 245764 | tf_op jit(solution)/shard_map/while
  97.3 7.0 copy-start.1
  124.7 7.0 copy-start.1
  147.7 9.7 copy-start.37
  162.2 54.8 %copy-start.36 = (f32[2,2,10,512]{3,2,1,0:T(8,128)S(1)}, f32[2,2,10,512]{3,2,1,0:T(8,128)}, u32[]{:S(2)}) copy-start(f32[2,2,10,512]{3,2,1,0:T(8,128)} %get-tuple-element.1077) | copy-start | bytes 245764 | tf_op jit(solution)/shard_map/while
  166.6 7.0 copy-start.1
  194.0 7.0 copy-start.1
  217.0 9.7 copy-start.37
  226.8 11.1 copy-start.34
  237.9 78.3 %copy-start.4 = (bf16[2048,640]{1,0:T(8,128)(2,1)S(1)}, bf16[2048,640]{1,0:T(8,128)(2,1)}, u32[]{:S(2)}) copy-start(bf16[2048,640]{1,0:T(8,128)(2,1)} %param.26) | copy-start | bytes 7864324
  237.9 78.3 %copy-start.40 = (f32[640]{0:T(1024)S(1)}, f32[640]{0:T(1024)}, u32[]{:S(2)}) copy-start(f32[640]{0:T(1024)} %get-tuple-element.569) | copy-start | bytes 7684
  242.7 123.9 %all-gather.5.cloned.1.call-start = ((), (), s32[]{:S(2)}) async-start(), calls=%async_computation.2 | async-start | bytes 3481600 | tf_op jit(solution)/shard_map/all_gather | solution.py:165
  243.4 247.0 %all-reduce.13.cloned.1.call-start = ((), (), s32[]{:S(2)}) async-start(), calls=%async_computation.3 | async-start | bytes 5242880 | tf_op jit(solution)/shard_map/psum | solution.py:216
  316.2 50.4 %copy-start.47 = (f32[640]{0:T(1024)S(1)}, f32[640]{0:T(1024)}, u32[]{:S(2)}) copy-start(f32[640]{0:T(1024)} %get-tuple-element.568) | copy-start | bytes 7684
  316.2 50.4 %copy-start.50 = (f32[1280]{0:T(1024)S(1)}, f32[1280]{0:T(1024)}, u32[]{:S(2)}) copy-start(f32[1280]{0:T(1024)} %param.32) | copy-start | bytes 15364
  316.2 50.4 %copy-start.58 = (f32[640]{0:T(1024)S(1)}, f32[640]{0:T(1024)}, u32[]{:S(2)}) copy-start(f32[640]{0:T(1024)} %get-tuple-element.567) | copy-start | bytes 7684
  366.6 31.1 %copy-start.27 = (bf16[2048,640]{1,0:T(8,128)(2,1)S(1)}, bf16[2048,640]{1,0:T(8,128)(2,1)}, u32[]{:S(2)}) copy-start(bf16[2048,640]{1,0:T(8,128)(2,1)} %param.27) | copy-start | bytes 7864324
  366.6 31.1 %copy-start.59 = (bf16[2,640,1280]{2,1,0:T(8,128)(2,1)S(1)}, bf16[2,640,1280]{2,1,0:T(8,128)(2,1)}, u32[]{:S(2)}) copy-start(bf16[2,640,1280]{2,1,0:T(8,128)(2,1)} %all-gather.5.cloned.1.call-done) | copy-start | bytes 9830404
  418.5 601.2 %all-reduce.15.cloned.1.call-start = ((), (), s32[]{:S(2)}) async-start(), calls=%async_computation.4 | async-start | bytes 20971520 | tf_op jit(solution)/shard_map/psum | solution.py:265
  418.5 7.4 copy-start.8
  418.5 7.4 copy-start.61
  527.2 7.0 copy-start
  557.0 14.6 %copy-start.2 = (bf16[2,512,10,32]{1,3,2,0:T(8,128)(2,1)S(1)}, bf16[2,512,10,32]{1,3,2,0:T(8,128)(2,1)}, u32[]{:S(2)}) copy-start(bf16[2,512,10,32]{1,3,2,0:T(8,128)(2,1)} %get-tuple-element.1029) | copy-start | bytes 1966084 | tf_op jit(solution)/shard_map/while/body/eval_jaxpr/while
  582.7 7.0 copy-start
  612.8 14.6 %copy-start.2 = (bf16[2,512,10,32]{1,3,2,0:T(8,128)(2,1)S(1)}, bf16[2,512,10,32]{1,3,2,0:T(8,128)(2,1)}, u32[]{:S(2)}) copy-start(bf16[2,512,10,32]{1,3,2,0:T(8,128)(2,1)} %get-tuple-element.1029) | copy-start | bytes 1966084 | tf_op jit(solution)/shard_map/while/body/eval_jaxpr/while
  665.5 7.0 copy-start
  695.3 14.6 %copy-start.2 = (bf16[2,512,10,32]{1,3,2,0:T(8,128)(2,1)S(1)}, bf16[2,512,10,32]{1,3,2,0:T(8,128)(2,1)}, u32[]{:S(2)}) copy-start(bf16[2,512,10,32]{1,3,2,0:T(8,128)(2,1)} %get-tuple-element.1029) | copy-start | bytes 1966084 | tf_op jit(solution)/shard_map/while/body/eval_jaxpr/while
  721.0 7.0 copy-start
  751.1 14.6 %copy-start.2 = (bf16[2,512,10,32]{1,3,2,0:T(8,128)(2,1)S(1)}, bf16[2,512,10,32]{1,3,2,0:T(8,128)(2,1)}, u32[]{:S(2)}) copy-start(bf16[2,512,10,32]{1,3,2,0:T(8,128)(2,1)} %get-tuple-element.1029) | copy-start | bytes 1966084 | tf_op jit(solution)/shard_map/while/body/eval_jaxpr/while
  787.6 8.3 copy-start.19
  787.6 8.3 copy-start.32
  817.1 335.7 %all-reduce.17.cloned.1.call-start = ((), (), s32[]{:S(2)}) async-start(), calls=%async_computation.5 | async-start | bytes 10485760 | tf_op jit(solution)/shard_map/psum | solution.py:201
  817.2 8.9 copy-start.18
  817.2 8.9 copy-start.35
  831.1 188.6 %copy-start.33 = (f32[4,40,320]{2,1,0:T(8,128)S(1)}, f32[4,40,320]{2,1,0:T(8,128)}, u32[]{:S(2)}) copy-start(f32[4,40,320]{2,1,0:T(8,128)} %param.29) | copy-start | bytes 614404
  831.1 191.8 %copy-start.26 = (f32[2,40,1280]{2,1,0:T(8,128)S(1)}, f32[2,40,1280]{2,1,0:T(8,128)}, u32[]{:S(2)}) copy-start(f32[2,40,1280]{2,1,0:T(8,128)} %param.30) | copy-start | bytes 1228804
  837.5 319.3 %copy-start.46 = (f32[2048]{0:T(1024)S(1)}, f32[2048]{0:T(1024)}, u32[]{:S(2)}) copy-start(f32[2048]{0:T(1024)} %copy-done.45) | copy-start | bytes 24580
  1156.2 131.7 %copy-start.41 = (f32[640]{0:T(1024)S(1)}, f32[640]{0:T(1024)}, u32[]{:S(2)}) copy-start(f32[640]{0:T(1024)} %get-tuple-element.569) | copy-start | bytes 7684
  (39 other events, 135.9 us)
Sparse Core Ops, SparseCore 0:
  10.9 40.9 all-gather.2
  242.8 73.3 all-reduce.10
  319.2 47.3 all-gather.4
  418.6 71.8 all-reduce.12
  817.2 202.3 all-reduce.14
  1022.7 130.0 all-reduce.16
where the time goes:
time: 1320 us; the launch traced here: 1300 us
  waiting for transfers between devices  519 us (39%)
  matrix products  279 us (21%)
  local copies, waits for them, and re-layouts  218 us (17%)
  other arithmetic  167 us (13%)
  blocking collectives  103 us (8%)
  between operations  17 us (1%)
    psum x1, waiting for transfers between devices, on_device(): lax.psum((grad_attn, grad_ffn, grad_head_bias, grad_hidden_bias, grad_vec...  182 us
    psum x1, waiting for transfers between devices, on_device(): lax.psum(jnp.einsum('tf,df->td', activated_low, gathered_ffn[1], preferre...  127 us
    psum x1, waiting for transfers between devices, on_device(): lax.psum(jnp.einsum('tw,dw->td', heads_low, out_projection, preferred_ele...  72.7 us
    dot_general x4, matrix products, attend_block_back(): jnp.einsum('qhd,khd->hqk', grad_heads, values_row, preferred_element_type...  60.6 us
    while x56, local copies, waits for them, and re-layouts  59.7 us
    convert_element_type x4, other arithmetic, attend_block_back(): grad_scores = (attention * (grad_attention - center)).astype(jnp.bfloat16)  58.3 us
    psum x1, waiting for transfers between devices, on_device(): lax.psum(jnp.einsum('tf,df->td', grad_pre, gathered_ffn[0], preferred_ele...  56.9 us
    psum x1, blocking collectives, on_device(): lax.psum((grad_attn, grad_ffn, grad_head_bias, grad_hidden_bias, grad_vec...  54 us
  transfers between devices with their start and end apart: 6, of which 6 were waited for; matrix products, arithmetic and copies ran while one was open for 4% of the time, Pallas kernels for 0%

commit v1 on v0

--- a/solution.py
+++ b/solution.py
@@ -13,6 +13,18 @@
 DECAY = 0.01
 RATE = 0.5
 MASKED = -1e30
+
+
+def doubled_up(x, axis, dim):
+    ways, here, hop = (lax.axis_size(axis), lax.axis_index(axis), x.shape[dim])
+    line, have = (x, 1)
+    while have < ways:
+        line = jnp.concatenate(
+            [line, lax.ppermute(line, axis, [(d, (d - have) % ways) for d in range(ways)])],
+            axis=dim,
+        )
+        have = 2 * have
+    return jnp.roll(line, here * hop, axis=dim)
 
 
 def layer_norm(values, scale_gain, offset):
@@ -162,7 +174,7 @@
     weight_sums = lax.psum(weight_terms, ("dp", "tp"))
     gathered_attn, gathered_ffn = (
         lax.all_gather(attn_weights.astype(jnp.bfloat16), "dp", axis=1, tiled=True),
-        lax.all_gather(ffn_weights.astype(jnp.bfloat16), "dp", axis=1, tiled=True),
+        doubled_up(ffn_weights.astype(jnp.bfloat16), "dp", 1),
     )
     tables = jax.vmap(rope_tables)(segment_ids)
     cosine_table = tables[0][:, :, None, :]

time: 1320 us -> 1350 us (1.023)
  local copies, waits for them, and re-layouts: 218 us -> 234 us
  waiting for transfers between devices: 519 us -> 534 us
    all_gather x1 -> x0, waiting for transfers between devices: 46.1 us -> none  [on_device(): lax.all_gather(ffn_weights.astype(jnp.bfloat16), 'dp', axis=1, tiled=True)]
    ppermute x0 -> x4, waiting for transfers between devices: none -> 24.9 us  [doubled_up(): lax.ppermute(line, axis, [(d, (d - have) % ways) for d in range(ways)])]
    psum x1, waiting for transfers between devices: 72.7 us -> 90.3 us  [on_device(): lax.psum(jnp.einsum('tw,dw->td', heads_low, out_projection, preferred_ele...]
    all_gather x1, waiting for transfers between devices: 34.1 us -> 50.7 us  [on_device(): lax.all_gather(attn_weights.astype(jnp.bfloat16), 'dp', axis=1, tiled=True)]
    unnamed x114 -> x136, local copies, waits for them, and re-layouts: 16.9 us -> 28.5 us
  transfers between devices with their start and end apart: 6 -> 9, of which waited for: 6 -> 8; matrix products, arithmetic and copies ran while one was open for 4% -> 17% of each run, Pallas kernels for 0% -> 0%
where the time goes in v1:
time: 1350 us
  waiting for transfers between devices  534 us (40%)
  matrix products  280 us (21%)
  local copies, waits for them, and re-layouts  234 us (17%)
  other arithmetic  172 us (13%)
  blocking collectives  103 us (8%)
  between operations  16.7 us (1%)
    psum x1, waiting for transfers between devices, on_device(): lax.psum((grad_attn, grad_ffn, grad_head_bias, grad_hidden_bias, grad_vec...  182 us
    psum x1, waiting for transfers between devices, on_device(): lax.psum(jnp.einsum('tf,df->td', activated_low, gathered_ffn[1], preferre...  127 us
    psum x1, waiting for transfers between devices, on_device(): lax.psum(jnp.einsum('tw,dw->td', heads_low, out_projection, preferred_ele...  90.3 us
    dot_general x4, matrix products, attend_block_back(): jnp.einsum('qhd,khd->hqk', grad_heads, values_row, preferred_element_type...  60.7 us
    while x56, local copies, waits for them, and re-layouts  59.7 us
    psum x1, waiting for transfers between devices, on_device(): lax.psum(jnp.einsum('tf,df->td', grad_pre, gathered_ffn[0], preferred_ele...  59 us
    convert_element_type x4, other arithmetic, attend_block_back(): grad_scores = (attention * (grad_attention - center)).astype(jnp.bfloat16)  58.3 us
    psum x1, blocking collectives, on_device(): lax.psum((grad_attn, grad_ffn, grad_head_bias, grad_hidden_bias, grad_vec...  54 us
  transfers between devices with their start and end apart: 9, of which 8 were waited for; matrix products, arithmetic and copies ran while one was open for 17% of the time, Pallas kernels for 0%

profile of v1, /device:TPU:12, one launch (start us, length us, event | category | flops | bytes accessed | tf_op | source)
XLA Modules:
  0.0 1347.1 jit_solution(351967213015380800)
XLA Ops:
  21.9 7.2 collective-permute-done.1
  34.3 16.3 %collective-permute-done.2 = bf16[2,160,1280]{2,1,0:T(8,128)(2,1)S(1)} collective-permute-done((bf16[2,160,1280]{2,1,0:T(8,128)(2,1)S(1)}, bf16[2,160,1280]{2,1,0:T(8,128)(2,1)S(1)}, u32[]{:S(2)}, u32[]{:S(2)}) %collective-permute-start.2) | collective-permute-done | bytes 819232 | tf_op jit(solution)/shard_map/ppermute | solution.py:23
  54.8 50.7 %all-gather.2.cloned.1.call-done = bf16[4,640,320]{2,0,1:T(4,128)(2,1)} async-done(((bf16[4,40,320]{2,0,1:T(4,128)(2,1)}), bf16[4,640,320]{2,0,1:T(4,128)(2,1)}) %all-gather.2.cloned.1.call-update) | async-done | bytes 1638416 | tf_op jit(solution)/shard_map/all_gather | solution.py:176
  117.9 8.1 slice.89
  138.0 139.4 %while.54 = (s32[]{:T(128)}, bf16[2,1024,10,32]{3,2,1,0:T(8,128)(2,1)}, f32[2,2,10,512]{3,2,1,0:T(8,128)}, bf16[2,1024,10,32]{1,3,2,0:T(8,128)(2,1)S(1)}, s32[2,...) while((s32[]{:T(128)}, ...), condition=%wide.region_8.9_spmd, body=%wide.region_3.8_spmd.sunk | while | flops 734522368 | bytes 181594624 | solution.py:193
  143.5 54.8 %while.57 = (s32[]{:T(128)}, bf16[2,512,10,32]{1,3,2,0:T(8,128)(2,1)S(1)}, f32[2,10,512]{2,1,0:T(8,128)S(1)}, s32[2,512]{1,0:T(2,128)S(1)}, s32[1024]{0:T(1024)S...) while((s32[]{:T(128)}, ...), condition=%wide.region_7.7_spmd, body=%wide.region_4.6_spmd.sunk | while | flops 734522368 | bytes 154048688 | solution.py:104
  147.9 7.0 copy-done.1
  154.9 6.2 fusion.167
  161.1 9.7 fusion.168
  175.3 7.0 copy-done.1
  182.3 6.2 fusion.167
  188.5 9.7 fusion.168
  212.9 54.8 %while.57 = (s32[]{:T(128)}, bf16[2,512,10,32]{1,3,2,0:T(8,128)(2,1)S(1)}, f32[2,10,512]{2,1,0:T(8,128)S(1)}, s32[2,512]{1,0:T(2,128)S(1)}, s32[1024]{0:T(1024)S...) while((s32[]{:T(128)}, ...), condition=%wide.region_7.7_spmd, body=%wide.region_4.6_spmd.sunk | while | flops 734522368 | bytes 154048688 | solution.py:104
  217.3 7.0 copy-done.1
  230.5 9.7 fusion.168
  244.7 7.0 copy-done.1
  257.9 9.7 fusion.168
  282.9 10.0 reshape.337
  311.8 90.3 %all-reduce.11.cloned.1.call-done = bf16[2048,640]{1,0:T(8,128)(2,1)} async-done(((bf16[2048,640]{1,0:T(8,128)(2,1)}), bf16[2048,640]{1,0:T(8,128)(2,1)}) %all-reduce.11.cloned.1.call-update) | async-done | bytes 2621456 | tf_op jit(solution)/shard_map/psum | solution.py:199
  406.6 31.5 %multiply_convert_fusion.1 = (bf16[2048,1280]{1,0:T(8,128)(2,1)}, f32[2048,1280]{1,0:T(8,128)}, f32[2048,1280]{1,0:T(8,128)}) fusion(f32[1280]{0:T(1024)S(1)} %copy-done.57, bf16[2,1280,1280]{2,1,0:T(8,128)(2,1)S(1)} %copy-done.63, s32[]{:T(128)S(6)} %select_n.25, f32[640]{0:T(1024)S(1)} %copy-done.66, f32[640]{0:T(1024)S(1)} %copy-done.54, ...), kind=kOutput, calls=%fused_computation.77 | convolution fusion | flops 3540254720 | bytes 33132548 | tf_op jit(solution)/shard_map/dot_general | solution.py:209
  438.1 12.6 convert_reduce_fusion
  459.1 7.3 convolution_bitcast_fusion
  474.0 59.0 %all-reduce.13.cloned.1.call-done = bf16[2048,640]{1,0:T(8,128)(2,1)} async-done(((bf16[2048,640]{1,0:T(8,128)(2,1)}), bf16[2048,640]{1,0:T(8,128)(2,1)}) %all-reduce.13.cloned.1.call-update) | async-done | bytes 2621456 | tf_op jit(solution)/shard_map/psum | solution.py:228
  553.1 277.1 %while.56 = (s32[]{:T(128)}, f32[2,1024,10,32]{1,3,2,0:T(8,128)}, f32[2,1024,10,32]{1,3,2,0:T(8,128)}, bf16[2,1024,10,32]{1,3,2,0:T(8,128)(2,1)}, bf16[2,1024,10...) while((s32[]{:T(128)}, f32[2,1024,10,32]{1,3,2,0:T(8,128)}, ...), condition=%wide.region_20.21_spmd, body=%wide.region_16.20_spmd.sunk | while | flops 1758686208 | bytes 284158464 | solution.py:244
  564.9 111.2 %while.58 = (s32[]{:T(128)}, f32[1024,10,32]{0,2,1:T(8,128)S(1)}, f32[1024,10,32]{0,2,1:T(8,128)}, f32[2,512,10,32]{1,3,2,0:T(8,128)}, bf16[2,512,10,32]{1,3,2,0...) while((s32[]{:T(128)}, f32[1024,10,32]{0,2,1:T(8,128)S(1)}, ...), condition=%wide.region_19.19_spmd.clone, body=%wide.region_17.18_spmd.clone.sunk | while | flops 1758686208 | bytes 255219920 | solution.py:122
  569.9 7.0 copy-done
  576.9 7.7 fusion.162
  584.5 15.2 %multiply_reduce_fusion.13 = (f32[10,512]{1,0:T(8,128)S(1)}, f32[10,512,1024]{2,1,0:T(8,128)}) fusion(f32[10,512,1024]{2,1,0:T(8,128)} %copy-done, f32[10,512]{1,0:T(8,128)S(1)} %dynamic-slice_bitcast_fusion.21, pred[512,1024]{1,0:T(8,128)(4,1)S(1)} %broadcast_compare_fusion.4, bf16[1024,10,32]{0,2,1:T(8,128)(2,1)} %get-tuple-element.1037, ...), kind=kOutput, calls=%fused_computation.18.clone.1 | convolution fusion | flops 361753600 | bytes 43491332 | tf_op jit(solution)/shard_map/while/body/eval_jaxpr/while/body/eval_jaxpr/qhd,khd->hqk/dot_general | solution.py:81
  599.7 14.6 %multiply_convert_fusion.3 = bf16[10,512,1024]{2,1,0:T(8,128)(2,1)S(1)} fusion(f32[10,512,1024]{2,1,0:T(8,128)} %get-tuple-element.989, f32[10,512,1024]{2,1,0:T(8,128)} %copy-done, f32[10,512]{1,0:T(8,128)S(1)} %get-tuple-element.990, f32[10,512]{1,0:T(8,128)S(1)} %dynamic-slice_bitcast_fusion.21, pred[512,1024]{1,0:T(8,128)(4,1)S(1)} %broadcast_compare_fusion.4), kind=kLoop, calls=%fused_computation.17.clone.1 | loop fusion | flops 31457280 | bytes 52994048 | tf_op jit(solution)/shard_map/while/body/eval_jaxpr/while/body/eval_jaxpr/convert_element_type | solution.py:85
  625.4 7.0 copy-done
  632.4 7.9 fusion.162
  640.3 15.2 %multiply_reduce_fusion.13 = (f32[10,512]{1,0:T(8,128)S(1)}, f32[10,512,1024]{2,1,0:T(8,128)}) fusion(f32[10,512,1024]{2,1,0:T(8,128)} %copy-done, f32[10,512]{1,0:T(8,128)S(1)} %dynamic-slice_bitcast_fusion.21, pred[512,1024]{1,0:T(8,128)(4,1)S(1)} %broadcast_compare_fusion.4, bf16[1024,10,32]{0,2,1:T(8,128)(2,1)} %get-tuple-element.1037, ...), kind=kOutput, calls=%fused_computation.18.clone.1 | convolution fusion | flops 361753600 | bytes 43491332 | tf_op jit(solution)/shard_map/while/body/eval_jaxpr/while/body/eval_jaxpr/qhd,khd->hqk/dot_general | solution.py:81
  655.5 14.6 %multiply_convert_fusion.3 = bf16[10,512,1024]{2,1,0:T(8,128)(2,1)S(1)} fusion(f32[10,512,1024]{2,1,0:T(8,128)} %get-tuple-element.989, f32[10,512,1024]{2,1,0:T(8,128)} %copy-done, f32[10,512]{1,0:T(8,128)S(1)} %get-tuple-element.990, f32[10,512]{1,0:T(8,128)S(1)} %dynamic-slice_bitcast_fusion.21, pred[512,1024]{1,0:T(8,128)(4,1)S(1)} %broadcast_compare_fusion.4), kind=kLoop, calls=%fused_computation.17.clone.1 | loop fusion | flops 31457280 | bytes 52994048 | tf_op jit(solution)/shard_map/while/body/eval_jaxpr/while/body/eval_jaxpr/convert_element_type | solution.py:85
  703.2 111.2 %while.58 = (s32[]{:T(128)}, f32[1024,10,32]{0,2,1:T(8,128)S(1)}, f32[1024,10,32]{0,2,1:T(8,128)}, f32[2,512,10,32]{1,3,2,0:T(8,128)}, bf16[2,512,10,32]{1,3,2,0...) while((s32[]{:T(128)}, f32[1024,10,32]{0,2,1:T(8,128)S(1)}, ...), condition=%wide.region_19.19_spmd.clone, body=%wide.region_17.18_spmd.clone.sunk | while | flops 1758686208 | bytes 255219920 | solution.py:122
  708.3 7.0 copy-done
  715.3 7.7 fusion.162
  722.9 15.2 %multiply_reduce_fusion.13 = (f32[10,512]{1,0:T(8,128)S(1)}, f32[10,512,1024]{2,1,0:T(8,128)}) fusion(f32[10,512,1024]{2,1,0:T(8,128)} %copy-done, f32[10,512]{1,0:T(8,128)S(1)} %dynamic-slice_bitcast_fusion.21, pred[512,1024]{1,0:T(8,128)(4,1)S(1)} %broadcast_compare_fusion.4, bf16[1024,10,32]{0,2,1:T(8,128)(2,1)} %get-tuple-element.1037, ...), kind=kOutput, calls=%fused_computation.18.clone.1 | convolution fusion | flops 361753600 | bytes 43491332 | tf_op jit(solution)/shard_map/while/body/eval_jaxpr/while/body/eval_jaxpr/qhd,khd->hqk/dot_general | solution.py:81
  738.1 14.6 %multiply_convert_fusion.3 = bf16[10,512,1024]{2,1,0:T(8,128)(2,1)S(1)} fusion(f32[10,512,1024]{2,1,0:T(8,128)} %get-tuple-element.989, f32[10,512,1024]{2,1,0:T(8,128)} %copy-done, f32[10,512]{1,0:T(8,128)S(1)} %get-tuple-element.990, f32[10,512]{1,0:T(8,128)S(1)} %dynamic-slice_bitcast_fusion.21, pred[512,1024]{1,0:T(8,128)(4,1)S(1)} %broadcast_compare_fusion.4), kind=kLoop, calls=%fused_computation.17.clone.1 | loop fusion | flops 31457280 | bytes 52994048 | tf_op jit(solution)/shard_map/while/body/eval_jaxpr/while/body/eval_jaxpr/convert_element_type | solution.py:85
  763.8 7.0 copy-done
  770.7 7.9 fusion.162
  778.7 15.2 %multiply_reduce_fusion.13 = (f32[10,512]{1,0:T(8,128)S(1)}, f32[10,512,1024]{2,1,0:T(8,128)}) fusion(f32[10,512,1024]{2,1,0:T(8,128)} %copy-done, f32[10,512]{1,0:T(8,128)S(1)} %dynamic-slice_bitcast_fusion.21, pred[512,1024]{1,0:T(8,128)(4,1)S(1)} %broadcast_compare_fusion.4, bf16[1024,10,32]{0,2,1:T(8,128)(2,1)} %get-tuple-element.1037, ...), kind=kOutput, calls=%fused_computation.18.clone.1 | convolution fusion | flops 361753600 | bytes 43491332 | tf_op jit(solution)/shard_map/while/body/eval_jaxpr/while/body/eval_jaxpr/qhd,khd->hqk/dot_general | solution.py:81
  793.8 14.6 %multiply_convert_fusion.3 = bf16[10,512,1024]{2,1,0:T(8,128)(2,1)S(1)} fusion(f32[10,512,1024]{2,1,0:T(8,128)} %get-tuple-element.989, f32[10,512,1024]{2,1,0:T(8,128)} %copy-done, f32[10,512]{1,0:T(8,128)S(1)} %get-tuple-element.990, f32[10,512]{1,0:T(8,128)S(1)} %dynamic-slice_bitcast_fusion.21, pred[512,1024]{1,0:T(8,128)(4,1)S(1)} %broadcast_compare_fusion.4), kind=kLoop, calls=%fused_computation.17.clone.1 | loop fusion | flops 31457280 | bytes 52994048 | tf_op jit(solution)/shard_map/while/body/eval_jaxpr/while/body/eval_jaxpr/convert_element_type | solution.py:85
  860.2 8.9 convolution_convert_fusion.1
  880.6 182.0 %all-reduce.15.cloned.1.call-done = (f32[4,640,320]{2,1,0:T(8,128)}, f32[2,640,1280]{2,1,0:T(8,128)}) async-done(((f32[4,640,320]{2,1,0:T(8,128)}, f32[2,640,1280]{2,1,0:T(8,128)}), (f32[4,640,320]{2,1,0:T(8,128)}, f32[2,640,1280]{2,1,0:T(8,128)})) %all-reduce.15.cloned.1.call-update) | async-done | bytes 9830416 | tf_op jit(solution)/shard_map/psum | solution.py:277
  1068.9 126.9 %all-reduce.17.cloned.1.call-done = (bf16[2048,640]{1,0:T(8,128)(2,1)}, bf16[2048,640]{1,0:T(8,128)(2,1)}) async-done(((bf16[2048,640]{1,0:T(8,128)(2,1)}, bf16[2048,640]{1,0:T(8,128)(2,1)}), (bf16[2048,640]{1,0:T(8,128)(2,1)}, bf16[2048,640]{1,0:T(8,128)(2,1)})) %all-reduce.17.cloned.1.call-update) | async-done | bytes 5242896 | tf_op jit(solution)/shard_map/psum | solution.py:213
  1204.9 54.0 %all-reduce.3 = (f32[3,320]{1,0:T(4,128)}, f32[1280]{0:T(1024)}, f32[6,640]{1,0:T(8,128)}) all-reduce(f32[3,320]{1,0:T(4,128)} %convert_reduce_fusion.2, f32[1280]{0:T(1024)} %get-tuple-element.701, f32[6,640]{1,0:T(8,128)S(1)} %stack.48), channel_id=1, replica_groups=mesh['dp'=16,'tp'=2] {'dp'}, use_global_device_ids=true, to_apply=%region_35.36 | all-reduce | flops 6080 | bytes 48640 | tf_op jit(solution)/shard_map/psum | solution.py:277
  1269.5 48.9 %all-reduce.2 = (f32[16]{0:T(128)}, f32[16]{0:T(128)}) all-reduce(f32[16]{0:T(128)} %concatenate.61, f32[16]{0:T(128)} %concatenate.59), channel_id=1, replica_groups=mesh['dp'=16,'tp'=2] {'dp','tp'}, use_global_device_ids=true, to_apply=%region_48.49 | all-reduce | flops 32 | bytes 256 | tf_op jit(solution)/shard_map/psum | solution.py:293
  1331.0 9.4 add_convert_fusion
  (396 shorter events, 348.5 us)
Async XLA Ops:
  7.2 25.5 %copy-start.3 = (bf16[2048,640]{1,0:T(8,128)(2,1)S(1)}, bf16[2048,640]{1,0:T(8,128)(2,1)}, u32[]{:S(2)}) copy-start(bf16[2048,640]{1,0:T(8,128)(2,1)} %param.26) | copy-start | bytes 7864324
  7.2 24.8 %copy-start.48 = (f32[6,640]{1,0:T(8,128)S(1)}, f32[6,640]{1,0:T(8,128)}, u32[]{:S(2)}) copy-start(f32[6,640]{1,0:T(8,128)} %param.33) | copy-start | bytes 46084
  7.2 98.3 %all-gather.2.cloned.1.call-start = ((), (), s32[]{:S(2)}) async-start(), calls=%async_computation | async-start | bytes 2088960 | tf_op jit(solution)/shard_map/all_gather | solution.py:176
  9.1 393.0 %all-reduce.11.cloned.1.call-start = ((), (), s32[]{:S(2)}) async-start(), calls=%async_computation.1 | async-start | bytes 5242880 | tf_op jit(solution)/shard_map/psum | solution.py:199
  10.9 41.9 %copy-start.27 = (bf16[2,40,1280]{2,1,0:T(8,128)(2,1)}, bf16[2,40,1280]{2,1,0:T(8,128)(2,1)S(1)}, u32[]{:S(2)}) copy-start(bf16[2,40,1280]{2,1,0:T(8,128)(2,1)S(1)} %get-tuple-element.676) | copy-start | bytes 614404
  10.9 4.1 collective-permute-start
  15.0 37.8 %copy-start.28 = (bf16[2,40,1280]{2,1,0:T(8,128)(2,1)}, bf16[2,40,1280]{2,1,0:T(8,128)(2,1)S(1)}, u32[]{:S(2)}) copy-start(bf16[2,40,1280]{2,1,0:T(8,128)(2,1)S(1)} %collective-permute-done) | copy-start | bytes 614404
  15.8 13.3 collective-permute-start.1
  21.8 88.2 %copy-start.58 = (f32[3,320]{1,0:T(4,128)S(1)}, f32[3,320]{1,0:T(4,128)}, u32[]{:S(2)}) copy-start(f32[3,320]{1,0:T(4,128)} %param.31) | copy-start | bytes 11524
  29.1 80.9 %copy-start.23 = (bf16[2,80,1280]{2,1,0:T(8,128)(2,1)}, bf16[2,80,1280]{2,1,0:T(8,128)(2,1)S(1)}, u32[]{:S(2)}) copy-start(bf16[2,80,1280]{2,1,0:T(8,128)(2,1)S(1)} %collective-permute-done.1) | copy-start | bytes 1228804
  29.2 21.4 %collective-permute-start.2 = (bf16[2,160,1280]{2,1,0:T(8,128)(2,1)S(1)}, bf16[2,160,1280]{2,1,0:T(8,128)(2,1)S(1)}, u32[]{:S(2)}, u32[]{:S(2)}) collective-permute-start(bf16[2,160,1280]{2,1,0:T(8,128)(2,1)S(1)} %pad_maximum_fusion.4), channel_id=1, source_target_pairs={{0,24},{2,26},{4,28},{6,30},{8,0},{10,2},{12,4},{14,6},{16,8},{18,... | collective-permute-start | bytes 2457608 | tf_op jit(solution)/shard_map/ppermute | solution.py:23
  32.6 82.2 %copy-start.55 = (f32[640]{0:T(1024)}, f32[640]{0:T(1024)S(1)}, u32[]{:S(2)}) copy-start(f32[640]{0:T(1024)S(1)} %get-tuple-element.571) | copy-start | bytes 7684
  32.6 82.2 %copy-start.64 = (f32[640]{0:T(1024)}, f32[640]{0:T(1024)S(1)}, u32[]{:S(2)}) copy-start(f32[640]{0:T(1024)S(1)} %get-tuple-element.570) | copy-start | bytes 7684
  32.7 82.2 %copy-start.44 = (f32[2048]{0:T(1024)}, f32[2048]{0:T(1024)S(1)}, u32[]{:S(2)}) copy-start(f32[2048]{0:T(1024)S(1)} %broadcast_multiply_fusion.2) | copy-start | bytes 24580
  34.3 80.7 %copy-start.50 = (f32[2048]{0:T(1024)}, f32[2048]{0:T(1024)S(1)}, u32[]{:S(2)}) copy-start(f32[2048]{0:T(1024)S(1)} %fusion.90) | copy-start | bytes 24580
  52.8 247.3 %collective-permute-start.3 = (bf16[2,320,1280]{2,1,0:T(8,128)(2,1)}, bf16[2,320,1280]{2,1,0:T(8,128)(2,1)}, u32[]{:S(2)}, u32[]{:S(2)}) collective-permute-start(bf16[2,320,1280]{2,1,0:T(8,128)(2,1)} %pad_maximum_fusion.3), channel_id=1, source_target_pairs={{0,16},{2,18},{4,20},{6,22},{8,24},{10,26},{12,28},{14,30},{16,0},... | collective-permute-start | bytes 4915208 | tf_op jit(solution)/shard_map/ppermute | solution.py:23
  143.5 54.8 %copy-start.42 = (f32[2,2,10,512]{3,2,1,0:T(8,128)S(1)}, f32[2,2,10,512]{3,2,1,0:T(8,128)}, u32[]{:S(2)}) copy-start(f32[2,2,10,512]{3,2,1,0:T(8,128)} %get-tuple-element.1079) | copy-start | bytes 245764 | tf_op jit(solution)/shard_map/while
  147.9 7.0 copy-start.1
  175.3 7.0 copy-start.1
  198.3 9.7 copy-start.43
  212.9 54.8 %copy-start.42 = (f32[2,2,10,512]{3,2,1,0:T(8,128)S(1)}, f32[2,2,10,512]{3,2,1,0:T(8,128)}, u32[]{:S(2)}) copy-start(f32[2,2,10,512]{3,2,1,0:T(8,128)} %get-tuple-element.1079) | copy-start | bytes 245764 | tf_op jit(solution)/shard_map/while
  217.3 7.0 copy-start.1
  244.7 7.0 copy-start.1
  267.7 9.8 copy-start.43
  277.5 15.4 %copy-start.12 = (bf16[2,1024,10,32]{1,3,2,0:T(8,128)(2,1)}, bf16[2,1024,10,32]{1,3,2,0:T(8,128)(2,1)S(1)}, u32[]{:S(2)}) copy-start(bf16[2,1024,10,32]{1,3,2,0:T(8,128)(2,1)S(1)} %get-tuple-element.1151) | copy-start | bytes 3932164
  282.9 10.0 copy-start.39
  297.6 235.5 %all-reduce.13.cloned.1.call-start = ((), (), s32[]{:S(2)}) async-start(), calls=%async_computation.2 | async-start | bytes 5242880 | tf_op jit(solution)/shard_map/psum | solution.py:228
  300.1 102.0 %copy-start.4 = (bf16[2048,640]{1,0:T(8,128)(2,1)S(1)}, bf16[2048,640]{1,0:T(8,128)(2,1)}, u32[]{:S(2)}) copy-start(bf16[2048,640]{1,0:T(8,128)(2,1)} %param.26) | copy-start | bytes 7864324
  300.1 102.0 %copy-start.46 = (f32[640]{0:T(1024)S(1)}, f32[640]{0:T(1024)}, u32[]{:S(2)}) copy-start(f32[640]{0:T(1024)} %get-tuple-element.569) | copy-start | bytes 7684
  406.6 31.5 %copy-start.32 = (bf16[2048,640]{1,0:T(8,128)(2,1)S(1)}, bf16[2048,640]{1,0:T(8,128)(2,1)}, u32[]{:S(2)}) copy-start(bf16[2048,640]{1,0:T(8,128)(2,1)} %param.27) | copy-start | bytes 7864324
  458.5 604.1 %all-reduce.15.cloned.1.call-start = ((), (), s32[]{:S(2)}) async-start(), calls=%async_computation.3 | async-start | bytes 20971520 | tf_op jit(solution)/shard_map/psum | solution.py:277
  459.0 7.4 copy-start.8
  459.0 7.4 copy-start.68
  569.9 7.0 copy-start
  599.7 14.6 %copy-start.2 = (bf16[2,512,10,32]{1,3,2,0:T(8,128)(2,1)S(1)}, bf16[2,512,10,32]{1,3,2,0:T(8,128)(2,1)}, u32[]{:S(2)}) copy-start(bf16[2,512,10,32]{1,3,2,0:T(8,128)(2,1)} %get-tuple-element.1031) | copy-start | bytes 1966084 | tf_op jit(solution)/shard_map/while/body/eval_jaxpr/while
  625.4 7.0 copy-start
  655.5 14.6 %copy-start.2 = (bf16[2,512,10,32]{1,3,2,0:T(8,128)(2,1)S(1)}, bf16[2,512,10,32]{1,3,2,0:T(8,128)(2,1)}, u32[]{:S(2)}) copy-start(bf16[2,512,10,32]{1,3,2,0:T(8,128)(2,1)} %get-tuple-element.1031) | copy-start | bytes 1966084 | tf_op jit(solution)/shard_map/while/body/eval_jaxpr/while
  738.1 14.6 %copy-start.2 = (bf16[2,512,10,32]{1,3,2,0:T(8,128)(2,1)S(1)}, bf16[2,512,10,32]{1,3,2,0:T(8,128)(2,1)}, u32[]{:S(2)}) copy-start(bf16[2,512,10,32]{1,3,2,0:T(8,128)(2,1)} %get-tuple-element.1031) | copy-start | bytes 1966084 | tf_op jit(solution)/shard_map/while/body/eval_jaxpr/while
  793.8 14.6 %copy-start.2 = (bf16[2,512,10,32]{1,3,2,0:T(8,128)(2,1)S(1)}, bf16[2,512,10,32]{1,3,2,0:T(8,128)(2,1)}, u32[]{:S(2)}) copy-start(bf16[2,512,10,32]{1,3,2,0:T(8,128)(2,1)} %get-tuple-element.1031) | copy-start | bytes 1966084 | tf_op jit(solution)/shard_map/while/body/eval_jaxpr/while
  830.2 8.3 copy-start.19
  830.2 8.3 copy-start.37
  860.1 335.7 %all-reduce.17.cloned.1.call-start = ((), (), s32[]{:S(2)}) async-start(), calls=%async_computation.4 | async-start | bytes 10485760 | tf_op jit(solution)/shard_map/psum | solution.py:213
  860.2 9.0 copy-start.18
  860.2 9.0 copy-start.41
  874.1 188.5 %copy-start.38 = (f32[4,40,320]{2,1,0:T(8,128)S(1)}, f32[4,40,320]{2,1,0:T(8,128)}, u32[]{:S(2)}) copy-start(f32[4,40,320]{2,1,0:T(8,128)} %param.29) | copy-start | bytes 614404
  874.1 191.7 %copy-start.31 = (f32[2,40,1280]{2,1,0:T(8,128)S(1)}, f32[2,40,1280]{2,1,0:T(8,128)}, u32[]{:S(2)}) copy-start(f32[2,40,1280]{2,1,0:T(8,128)} %param.30) | copy-start | bytes 1228804
  880.6 319.2 %copy-start.53 = (f32[2048]{0:T(1024)S(1)}, f32[2048]{0:T(1024)}, u32[]{:S(2)}) copy-start(f32[2048]{0:T(1024)} %copy-done.52) | copy-start | bytes 24580
  1199.2 131.8 %copy-start.47 = (f32[640]{0:T(1024)S(1)}, f32[640]{0:T(1024)}, u32[]{:S(2)}) copy-start(f32[640]{0:T(1024)} %get-tuple-element.569) | copy-start | bytes 7684
  (49 other events, 181.3 us)
Sparse Core Ops, SparseCore 0:
  10.9 94.5 all-gather.1
  297.7 104.3 all-reduce.10
  458.7 74.3 all-reduce.12
  860.2 202.3 all-reduce.14
  1065.7 130.0 all-reduce.16
